TPU v7x, 256 devices: a whole 4x4x8 slice. The times are simulated.
256 devices in a mesh: dp: 32 (over y, x, core), vocab: 8 (over z).
Axes of the slice: x: 4, y: 4, z: 8, core: 2. Of those that a mesh axis runs over, the one named last changes fastest.
Arguments:
- hidden_states: float32 [24576, 2048], P('dp'), may hold values from -8 to 8
- norm_gain: float32 [2048], replicated, may hold values from 0.5 to 1.5
- head_weight: bfloat16 [32768, 2048], P(('vocab', 'dp')), may hold values from -2 to 2
- target_ids: int32 [24576], P('dp'), may hold values from 0 to 32767
- lengths: int32 [32], P('dp'), may hold values from 1 to 768, as said below
Outputs:
- log_probs: float32 [24576], P('dp')
- entropies: float32 [24576], P('dp')
Inputs may be any that keep to these rules, and one draw needn't show every extreme that they name: `lengths`: live tokens of a sequence; some sequence fills all 768 slots.
All inputs are finite; a program needn't handle non-finite values.
Results may differ from a plain program's by a relative error of at most 0.0015.
Values may be sent and summed in bfloat16 or wider, within the bound.
No kernel may reach another device: no remote copies, remote signals or barrier semaphores. Data moves between devices by JAX's collectives and lax.ppermute only.
A program may use at most 128 MiB of HBM per device.

v0:
```python
import jax
import jax.numpy as jnp
from jax import lax
from jax.sharding import PartitionSpec as P

epsilon = 1e-05
lowest = -1e30


def score_piece(normed, shard_piece):
    return lax.dot_general(
        normed, shard_piece, (((1,), (1,)), ((), ())), preferred_element_type=jnp.float32
    )


def update_stats(carry, logits, goal_cols):
    maxima, totals, tilted, target_logit = carry
    columns = jnp.arange(logits.shape[1], dtype=jnp.int32)
    highest = jnp.maximum(maxima, jnp.max(logits, axis=1))
    weights = jnp.exp(logits - highest[:, None])
    totals = jnp.sum(weights, axis=1)
    tilted = jnp.sum(weights * logits, axis=1)
    matched = jnp.where(columns[None, :] == goal_cols[:, None], logits, 0.0)
    target_logit = jnp.sum(matched, axis=1)
    return (highest, totals, tilted, target_logit)


def on_device(hidden_states, norm_gain, head_weight, target_ids, lengths):
    row_count = hidden_states.shape[0]
    scale = lax.rsqrt(jnp.mean(hidden_states * hidden_states, axis=1, keepdims=True) + epsilon)
    normed = (hidden_states * scale * norm_gain).astype(jnp.bfloat16)
    slice_width = head_weight.shape[0] * lax.axis_size("dp")
    goal_cols = target_ids - lax.axis_index("vocab") * slice_width
    live_count = lengths[0]
    positions = jnp.arange(row_count, dtype=jnp.int32)
    live_mask = positions < live_count
    initial = (
        jnp.full((row_count,), lowest, jnp.float32),
        jnp.zeros((row_count,), jnp.float32),
        jnp.zeros((row_count,), jnp.float32),
        jnp.zeros((row_count,), jnp.float32),
    )
    logits = score_piece(normed, lax.all_gather(head_weight, "dp", axis=0, tiled=True))
    stats = update_stats(initial, logits, goal_cols)
    maxima = lax.pmax(stats[0], "vocab")
    factor = jnp.exp(stats[0] - maxima)
    totals, tilted, target_logit = lax.psum(
        (stats[1] * factor, stats[2] * factor, stats[3]), "vocab"
    )
    log_total = maxima + jnp.log(totals)
    log_probs = jnp.where(live_mask, target_logit - log_total, 0.0)
    entropies = jnp.where(live_mask, log_total - tilted / totals, 0.0)
    return (log_probs, entropies)


def solution(mesh):
    in_specs = (P("dp", None), P(), P(("vocab", "dp"), None), P("dp"), P("dp"))
    out_specs = (P("dp"), P("dp"))
    return jax.shard_map(
        on_device, mesh=mesh, in_specs=in_specs, out_specs=out_specs, check_vma=False
    )
```

profile of v0, /device:TPU:2, one launch (start us, length us, event | category | flops | bytes accessed | tf_op | source)
XLA Modules:
  0.0 172.5 jit_solution(5510616393231229404)
XLA Ops:
  7.2 0.0 all-gather.2.cloned.1.call-start
  7.2 0.7 all-gather.2.cloned.1.call-update
  8.5 3.3 %multiply_reduce_fusion.1 = f32[768]{0:T(1024)S(1)} fusion(f32[768,2048]{1,0:T(8,128)} %param.5), kind=kLoop, calls=%fused_computation.6 | loop fusion | flops 3144960 | bytes 6294528 | tf_op jit(solution)/shard_map/reduce_sum | solution.py:30
  11.8 0.7 broadcast_subtract_fusion
  12.5 78.5 %all-gather.2.cloned.1.call-done = bf16[4096,2048]{1,0:T(8,128)(2,1)} async-done(((bf16[128,2048]{1,0:T(8,128)(2,1)}), bf16[4096,2048]{1,0:T(8,128)(2,1)}) %all-gather.2.cloned.1.call-update) | async-done | bytes 16777232 | tf_op jit(solution)/shard_map/all_gather | solution.py:43
  91.1 21.3 %fusion.6 = (f32[768]{0:T(1024)S(1)}, f32[768,4096]{1,0:T(8,128)}) fusion(bf16[4096,2048]{1,0:T(8,128)(2,1)} %all-gather.2.cloned.1.call-done, f32[768,2048]{1,0:T(8,128)} %param.5, f32[2048]{0:T(1024)} %param.6, f32[768]{0:T(1024)S(1)} %add_rsqrt_fusion), kind=kOutput, calls=%fused_computation.20 | convolution fusion | flops 12892765184 | bytes 35665920 | tf_op jit(solution)/shard_map/dot_general | solution.py:11
  112.4 17.5 %pmax.7 = f32[768]{0:T(1024)S(1)} all-reduce(f32[768]{0:T(1024)S(1)} %broadcast_maximum_fusion), channel_id=1, replica_groups=mesh['dp'=32,'vocab'=8] {'vocab'}, use_global_device_ids=true, to_apply=%region_4.5 | all-reduce | flops 768 | bytes 6144 | tf_op jit(solution)/shard_map/pmax | solution.py:45
  129.8 7.4 %multiply_reduce_fusion = (f32[768]{0:T(1024)S(1)}, f32[768]{0:T(1024)S(1)}, f32[768]{0:T(1024)S(1)}) fusion(f32[768,4096]{1,0:T(8,128)} %get-tuple-element.13, f32[768]{0:T(1024)S(1)} %broadcast_maximum_fusion, s32[768]{0:T(1024)S(1)} %broadcast_subtract_fusion), kind=kLoop, calls=%fused_computation | loop fusion | flops 22017792 | bytes 12598272 | tf_op jit(solution)/shard_map/reduce_sum | solution.py:22
  137.3 27.8 %all-reduce = (f32[768]{0:T(1024)S(1)}, f32[768]{0:T(1024)S(1)}, f32[768]{0:T(1024)S(1)}) all-reduce(f32[768]{0:T(1024)S(1)} %get-tuple-element.4, f32[768]{0:T(1024)S(1)} %get-tuple-element.11, f32[768]{0:T(1024)S(1)} %get-tuple-element.10), channel_id=1, replica_groups=mesh['dp'=32,'vocab'=8] {'vocab'}, use_global_device_ids=true, to_apply=%region_2.0 | all-reduce | flops 2304 | bytes 18432 | tf_op jit(solution)/shard_map/psum | solution.py:47
  165.0 0.6 subtract_select_fusion
  (3 shorter events, 0.0 us)
Async XLA Ops:
  7.2 83.9 %all-gather.2.cloned.1.call-start = ((), (), s32[]{:S(2)}) async-start(), calls=%async_computation | async-start | bytes 17301504 | tf_op jit(solution)/shard_map/all_gather | solution.py:43
Sparse Core Ops, SparseCore 0:
  10.5 80.4 all-gather.1
where the time goes:
time: 173 us; the launch traced here: 172 us
  waiting for transfers between devices  79.2 us (46%)
  blocking collectives  45.2 us (26%)
  matrix products  21.3 us (12%)
  between operations  14.7 us (8%)
  other arithmetic  12 us (7%)
    all_gather x1, waiting for transfers between devices, on_device(): lax.all_gather(head_weight, 'dp', axis=0, tiled=True)  78.5 us
    psum x1, blocking collectives, on_device(): lax.psum((stats[1] * factor, stats[2] * factor, stats[3]), 'vocab')  27.8 us
    dot_general x1, matrix products, score_piece(): lax.dot_general(normed, shard_piece, (((1,), (1,)), ((), ())), preferred_...  21.3 us
    pmax x1, blocking collectives, on_device(): maxima = lax.pmax(stats[0], 'vocab')  17.5 us
    reduce_sum x1, other arithmetic, update_stats(): tilted = jnp.sum(weights * logits, axis=1)  7.43 us
  transfers between devices with their start and end apart: 1, of which 1 were waited for; matrix products, arithmetic and copies ran while one was open for 2% of the time, Pallas kernels for 0%

commit v1 on v0

v1 whole, which is shorter than its diff:
```python
import functools

import jax
import jax.numpy as jnp
from jax import lax
from jax.experimental import pallas as pl
from jax.experimental.pallas import tpu as pltpu
from jax.sharding import PartitionSpec as P


epsilon = 1e-05
lowest = -1e30


SIDE = 4
BLOCK = 256


def index_of(y, x, core):
    return ((y % SIDE) * SIDE + x % SIDE) * 2 + core


def shift(value, dy, dx):
    pairs = [
        (index_of(y, x, c), index_of(y + dy, x + dx, c))
        for y in range(SIDE)
        for x in range(SIDE)
        for c in range(2)
    ]
    return lax.ppermute(value, "dp", pairs)


def swap_cores(value):
    return lax.ppermute(value, "dp", [(i, i ^ 1) for i in range(2 * SIDE * SIDE)])


def norm_kernel(h_ref, g_ref, o_ref):
    h = h_ref[...]
    scale = lax.rsqrt(jnp.mean(h * h, axis=1, keepdims=True) + epsilon)
    o_ref[0] = (h * scale * g_ref[...]).astype(jnp.bfloat16).T


def normalize(hidden_states, norm_gain):
    rows, width = hidden_states.shape
    return pl.pallas_call(
        norm_kernel,
        grid=(rows // BLOCK,),
        in_specs=[
            pl.BlockSpec((BLOCK, width), lambda i: (i, 0)),
            pl.BlockSpec((1, width), lambda i: (0, 0)),
        ],
        out_specs=pl.BlockSpec((1, width, BLOCK), lambda i: (i, 0, 0)),
        out_shape=jax.ShapeDtypeStruct((rows // BLOCK, width, BLOCK), jnp.bfloat16),
        cost_estimate=pl.CostEstimate(flops=4 * rows * width, bytes_accessed=6 * rows * width, transcendentals=rows),
        name="normalize",
    )(hidden_states, norm_gain.reshape(1, width))


def score_kernel(heights, spans, chunk, last, place_ref, goal_ref, prev_ref, own_ref, other_ref, *refs):
    count = len(heights)
    pieces, refs = refs[:count], refs[count:]
    outs, refs = (refs[:2], refs[2:]) if last else (refs[:1], refs[1:])
    rows_ref, tokens_ref, rows_sem, tokens_sem = refs
    mine = own_ref.shape[0]
    blocks = 2 * mine

    at = 0
    row_copies = []
    for k, (piece, height) in enumerate(zip(pieces, heights)):
        row_copies.append(pltpu.make_async_copy(piece, rows_ref.at[pl.ds(at, height)], rows_sem.at[k]))
        at += height
    for copy in row_copies:
        copy.start()

    def fetch(source, block, slot):
        return pltpu.make_async_copy(source.at[block], tokens_ref.at[slot], tokens_sem.at[slot])

    fetch(own_ref, 0, 0).start()
    for copy in row_copies:
        copy.wait()
    first, y, x, core = place_ref[0], place_ref[1], place_ref[2], place_ref[3]
    bases = []
    for dy, dx, offset, _ in spans:
        owner = (((y + dy) & (SIDE - 1)) * SIDE + ((x + dx) & (SIDE - 1))) * 2 + core
        bases.append(first + owner * chunk + offset)

    def step(i, carry):
        slot = lax.rem(i, 2)
        after = i + 1

        @pl.when(after < mine)
        def _():
            fetch(own_ref, after, 1 - slot).start()

        @pl.when((after >= mine) & (after < blocks))
        def _():
            fetch(other_ref, after - mine, 1 - slot).start()

        fetch(own_ref, 0, slot).wait()
        logits = jnp.dot(rows_ref[...], tokens_ref[slot], preferred_element_type=jnp.float32)
        prev = prev_ref[i]
        old = prev[0:1]
        highest = jnp.maximum(old, jnp.max(logits, axis=0, keepdims=True))
        weights = jnp.exp(logits - highest)
        factor = jnp.exp(old - highest)
        totals = prev[1:2] * factor + jnp.sum(weights, axis=0, keepdims=True)
        tilted = prev[2:3] * factor + jnp.sum(weights * logits, axis=0, keepdims=True)
        goal = goal_ref[i]
        target = prev[3:4]
        at = 0
        for base, (_, _, _, span) in zip(bases, spans):
            part = logits[at : at + span]
            line = lax.broadcasted_iota(jnp.int32, part.shape, 0)
            target = target + jnp.sum(jnp.where(line == goal - base, part, 0.0), axis=0, keepdims=True)
            at += span

        def write(ref, block):
            ref[block, 0:1, :] = highest
            ref[block, 1:2, :] = totals
            ref[block, 2:3, :] = tilted
            ref[block, 3:4, :] = target

        if last:

            @pl.when(i < mine)
            def _():
                write(outs[0], i)

            @pl.when(i >= mine)
            def _():
                write(outs[1], i - mine)

        else:
            write(outs[0], i)
        return carry

    lax.fori_loop(0, blocks, step, 0)


def score(place, goals, prev, own, other, chunk, pieces, last=False):
    values = [value for value, _ in pieces]
    spans = tuple(span for _, names in pieces for span in names)
    heights = tuple(v.shape[0] for v in values)
    total, (mine, width, block) = sum(heights), own.shape
    slots = 2 * mine * block
    if last:
        out_shape = [jax.ShapeDtypeStruct((mine, 4, block), jnp.float32)] * 2
    else:
        out_shape = [jax.ShapeDtypeStruct((2 * mine, 4, block), jnp.float32)]
    anywhere = pl.BlockSpec(memory_space=pl.ANY)
    local = pl.BlockSpec(memory_space=pltpu.VMEM)
    return pl.pallas_call(
        functools.partial(score_kernel, heights, spans, chunk, last),
        in_specs=[pl.BlockSpec(memory_space=pltpu.SMEM), local, local, anywhere, anywhere]
        + [anywhere] * len(values),
        out_specs=[local] * len(out_shape),
        out_shape=out_shape,
        scratch_shapes=[
            pltpu.VMEM((total, width), jnp.bfloat16),
            pltpu.VMEM((2, width, block), jnp.bfloat16),
            pltpu.SemaphoreType.DMA((len(values),)),
            pltpu.SemaphoreType.DMA((2,)),
        ],
        compiler_params=pltpu.CompilerParams(vmem_limit_bytes=24 << 20),
        cost_estimate=pl.CostEstimate(
            flops=2 * total * slots * width,
            bytes_accessed=2 * (total + slots) * width,
            transcendentals=total * slots,
        ),
        name="score",
    )(place, goals, prev, own, other, *values)


def fold(parts):
    highest = functools.reduce(jnp.maximum, [p[:, 0:1] for p in parts])
    factors = [jnp.exp(p[:, 0:1] - highest) for p in parts]
    totals = sum(p[:, 1:2] * f for p, f in zip(parts, factors))
    tilted = sum(p[:, 2:3] * f for p, f in zip(parts, factors))
    target = sum(p[:, 3:4] for p in parts)
    return highest, totals, tilted, target


def merge_kernel(a_ref, b_ref, o_ref):
    for k, value in enumerate(fold([a_ref[...], b_ref[...]])):
        o_ref[:, k : k + 1, :] = value


def merge(a, b):
    return pl.pallas_call(merge_kernel, out_shape=jax.ShapeDtypeStruct(a.shape, a.dtype), name="merge")(a, b)


def finish_kernel(length_ref, *refs):
    parts, (log_probs_ref, entropies_ref) = refs[:-2], refs[-2:]
    highest, totals, tilted, target = fold([p[...] for p in parts])
    log_total = highest + jnp.log(totals)
    block = lax.broadcasted_iota(jnp.int32, highest.shape, 0)
    slot = lax.broadcasted_iota(jnp.int32, highest.shape, 2)
    live = block * highest.shape[2] + slot < length_ref[0]
    log_probs_ref[...] = jnp.where(live, target - log_total, 0.0)
    entropies_ref[...] = jnp.where(live, log_total - tilted / totals, 0.0)


def finish(lengths, parts):
    blocks, _, block = parts[0].shape
    local = pl.BlockSpec(memory_space=pltpu.VMEM)
    return pl.pallas_call(
        finish_kernel,
        in_specs=[pl.BlockSpec(memory_space=pltpu.SMEM)] + [local] * len(parts),
        out_specs=[local] * 2,
        out_shape=[jax.ShapeDtypeStruct((blocks, 1, block), jnp.float32)] * 2,
        name="finish",
    )(lengths, *parts)


def on_device(hidden_states, norm_gain, head_weight, target_ids, lengths):
    row_count = hidden_states.shape[0]
    chunk = head_weight.shape[0]
    h, q = chunk // 2, chunk // 4
    mine = row_count // BLOCK
    device = lax.axis_index("dp")
    core, x, y = device % 2, (device // 2) % SIDE, device // (2 * SIDE)
    first_row = lax.axis_index("vocab") * (chunk * lax.axis_size("dp"))
    place = jnp.stack([first_row, y, x, core])
    cat = lambda *v: jnp.concatenate(v, axis=0)
    a = lambda dy, dx, lo, size: (dy, dx, lo, size)
    b = lambda dy, dx, lo, size: (dy, dx, h + lo, size)

    own = head_weight
    left, right = shift(own, 0, 1), shift(own, 0, -1)
    down, up = shift(own, 1, 0), shift(own, -1, 0)
    tokens = normalize(hidden_states, norm_gain)
    others = swap_cores(tokens)
    goals = cat(target_ids, swap_cores(target_ids)).reshape(2 * mine, 1, BLOCK)

    f_xp = shift(cat(down[h : h + q], up[h : h + q], left[:q], left[h : h + q]), 0, 1)
    f_xm = shift(cat(down[h + q :], up[h + q :], right[q:h], right[h + q :]), 0, -1)
    f_yp = shift(cat(left[:q], right[:q], down[h : h + q], down[:q]), 1, 0)
    f_ym = shift(cat(left[q:h], right[q:h], up[h + q :], up[q:h]), -1, 0)
    g_xp = shift(cat(down[h + q :], up[h + q :]), 0, 1)
    g_xm = shift(cat(down[h : h + q], up[h : h + q]), 0, -1)
    g_yp = shift(cat(left[q:h], right[q:h]), 1, 0)
    g_ym = shift(cat(left[:q], right[:q]), -1, 0)
    initial = cat(jnp.full((1, 1), lowest, jnp.float32), jnp.zeros((3, 1), jnp.float32))
    initial = jnp.broadcast_to(initial, (2 * mine, 4, BLOCK))
    fold_in = functools.partial(score, place, goals, own=tokens, other=others, chunk=chunk)
    whole = lambda dy, dx: [(dy, dx, 0, chunk)]
    (stats,) = fold_in(
        initial,
        pieces=[
            (own, whole(0, 0)),
            (left, whole(0, -1)),
            (right, whole(0, 1)),
            (down, whole(-1, 0)),
            (up, whole(1, 0)),
        ],
    )

    a2_low, a2_high = f_xp[2 * q : 3 * q], f_xm[2 * q : 3 * q]
    b2_low, b2_high = f_yp[2 * q : 3 * q], f_ym[2 * q : 3 * q]
    p_yp, p_ym = shift(a2_low, 1, 0), shift(a2_high, -1, 0)
    p_xp, p_xm = shift(b2_low, 0, 1), shift(b2_high, 0, -1)
    q_yp = shift(cat(a2_high, f_yp[: 2 * q]), 1, 0)
    q_ym = shift(cat(a2_low, f_ym[: 2 * q]), -1, 0)
    q_xp = shift(cat(b2_high, f_xp[: 2 * q]), 0, 1)
    q_xm = shift(cat(b2_low, f_xm[: 2 * q]), 0, -1)
    r_yp, r_ym = shift(p_yp, 1, 0), shift(p_ym, -1, 0)
    r_xp, r_xm = shift(p_xp, 0, 1), shift(p_xm, 0, -1)
    (stats,) = fold_in(
        stats,
        pieces=[
            (f_xp, [b(-1, -1, 0, q), b(1, -1, 0, q), a(0, 2, 0, q), b(0, 2, 0, q)]),
            (f_xm, [b(-1, 1, q, q), b(1, 1, q, q), a(0, 2, q, q), b(0, 2, q, q)]),
            (f_yp, [a(-1, -1, 0, q), a(-1, 1, 0, q), b(2, 0, 0, q), a(2, 0, 0, q)]),
            (f_ym, [a(1, -1, q, q), a(1, 1, q, q), b(2, 0, q, q), a(2, 0, q, q)]),
            (g_xp, [b(-1, -1, q, q), b(1, -1, q, q)]),
            (g_xm, [b(-1, 1, 0, q), b(1, 1, 0, q)]),
            (g_yp, [a(-1, -1, q, q), a(-1, 1, q, q)]),
            (g_ym, [a(1, -1, 0, q), a(1, 1, 0, q)]),
            (p_yp, [a(-1, 2, 0, q)]),
            (p_ym, [a(1, 2, q, q)]),
            (p_xp, [b(2, -1, 0, q)]),
            (p_xm, [b(2, 1, q, q)]),
        ],
    )
    ours, theirs = fold_in(
        stats,
        pieces=[
            (q_yp, [a(-1, 2, q, q), a(2, -1, 0, q), a(2, 1, 0, q)]),
            (q_ym, [a(1, 2, 0, q), a(2, -1, q, q), a(2, 1, q, q)]),
            (q_xp, [b(2, -1, q, q), b(-1, 2, 0, q), b(1, 2, 0, q)]),
            (q_xm, [b(2, 1, 0, q), b(-1, 2, q, q), b(1, 2, q, q)]),
            (r_yp, [a(2, 2, 0, q)]),
            (r_ym, [a(2, 2, q, q)]),
            (r_xp, [b(2, 2, 0, q)]),
            (r_xm, [b(2, 2, q, q)]),
        ],
        last=True,
    )

    ours = merge(ours, swap_cores(theirs))
    depth = lax.axis_size("vocab")
    forth = [(i, (i + 1) % depth) for i in range(depth)]
    back = [(i, (i - 1) % depth) for i in range(depth)]
    parts = [ours]
    rising = falling = ours
    for step in range(depth // 2):
        rising = lax.ppermute(rising, "vocab", forth)
        parts.append(rising)
        if step < depth // 2 - 1:
            falling = lax.ppermute(falling, "vocab", back)
            parts.append(falling)
    log_probs, entropies = finish(lengths, parts)
    return (log_probs.reshape(row_count), entropies.reshape(row_count))


def solution(mesh):
    in_specs = (P("dp", None), P(), P(("vocab", "dp"), None), P("dp"), P("dp"))
    out_specs = (P("dp"), P("dp"))
    return jax.shard_map(on_device, mesh=mesh, in_specs=in_specs, out_specs=out_specs, check_vma=False)
```

time: 173 us -> 116 us (0.67)
  waiting for transfers between devices: 79.2 us -> 21.8 us
  starting transfers between devices: 0.04 us -> 50.4 us
  blocking collectives: 45.2 us -> 0 us
  Pallas kernels: 0 us -> 35.7 us
  matrix products: 21.3 us -> 0 us
  between operations: 14.7 us -> 1.68 us
  other arithmetic: 12 us -> 1.81 us
  local copies, waits for them, and re-layouts: 0 us -> 4.03 us
    all_gather x1 -> x0, waiting for transfers between devices: 78.5 us -> none  [on_device(): lax.all_gather(head_weight, 'dp', axis=0, tiled=True)]
    ppermute x0 -> x34, starting transfers between devices: none -> 50.4 us  [the longest x24 37.4 us: shift(): return lax.ppermute(value, 'dp', pairs)]
    pallas_call x0 -> x6, Pallas kernels: none -> 35.7 us  [the longest x3 27 us: score(): pl.pallas_call(functools.partial(score_kernel, heights, spans, chunk, las...]
    psum x1 -> x0, blocking collectives: 27.8 us -> none  [on_device(): lax.psum((stats[1] * factor, stats[2] * factor, stats[3]), 'vocab')]
    ppermute x0 -> x34, waiting for transfers between devices: none -> 21.8 us  [the longest x24 11.2 us: shift(): return lax.ppermute(value, 'dp', pairs)]
    dot_general x1 -> x0, matrix products: 21.3 us -> none  [score_piece(): lax.dot_general(normed, shard_piece, (((1,), (1,)), ((), ())), preferred_...]
    pmax x1 -> x0, blocking collectives: 17.5 us -> none  [on_device(): maxima = lax.pmax(stats[0], 'vocab')]
    reduce_sum x2 -> x0, other arithmetic: 10.7 us -> none  [the longest x1 7.43 us: update_stats(): tilted = jnp.sum(weights * logits, axis=1)]
  transfers between devices with their start and end apart: 1 -> 34, of which waited for: 1 -> 11; matrix products, arithmetic and copies ran while one was open for 2% -> 1% of each run, Pallas kernels for 0% -> 21%
where the time goes in v1:
time: 116 us; the launch traced here: 115 us
  starting transfers between devices  50.4 us (43%)
  Pallas kernels  35.7 us (31%)
  waiting for transfers between devices  21.8 us (19%)
  local copies, waits for them, and re-layouts  4.03 us (3%)
  other arithmetic  1.81 us (2%)
  between operations  1.68 us (1%)
    ppermute x24, starting transfers between devices, shift(): return lax.ppermute(value, 'dp', pairs)  37.4 us
    pallas_call x3, Pallas kernels, score(): pl.pallas_call(functools.partial(score_kernel, heights, spans, chunk, las...  27 us
    ppermute x24, waiting for transfers between devices, shift(): return lax.ppermute(value, 'dp', pairs)  11.2 us
    ppermute x3, starting transfers between devices, on_device(): falling = lax.ppermute(falling, 'vocab', back)  10.4 us
    ppermute x4, waiting for transfers between devices, on_device(): rising = lax.ppermute(rising, 'vocab', forth)  9.43 us
    pallas_call x1, Pallas kernels, normalize(): pl.pallas_call(norm_kernel, grid=(rows // BLOCK,), in_specs=[pl.BlockSpec...  5.94 us
  transfers between devices with their start and end apart: 34, of which 11 were waited for; matrix products, arithmetic and copies ran while one was open for 1% of the time, Pallas kernels for 21%

profile of v1, /device:TPU:2, one launch (start us, length us, event | category | flops | bytes accessed | tf_op | source)
XLA Modules:
  0.0 115.4 jit_solution(6074421099034149704)
XLA Ops:
  0.6 1.7 %collective-permute-start.4 = (bf16[128,2048]{1,0:T(8,128)(2,1)}, bf16[128,2048]{1,0:T(8,128)(2,1)S(1)}, u32[]{:S(2)}, u32[]{:S(2)}) collective-permute-start(bf16[128,2048]{1,0:T(8,128)(2,1)} %refs_0_.1), channel_id=1, source_target_pairs={{0,64},{8,72},{16,80},{24,88},{32,96},{40,104},{48,112},{56,120},{... | collective-permute-start | bytes 1572872 | tf_op jit(solution)/shard_map/ppermute | solution.py:30
  2.3 1.5 %collective-permute-start.2 = (bf16[128,2048]{1,0:T(8,128)(2,1)}, bf16[128,2048]{1,0:T(8,128)(2,1)S(1)}, u32[]{:S(2)}, u32[]{:S(2)}) collective-permute-start(bf16[128,2048]{1,0:T(8,128)(2,1)} %refs_0_.1), channel_id=1, source_target_pairs={{0,16},{8,24},{16,32},{24,40},{32,48},{40,56},{48,0},{56,8},{64,80... | collective-permute-start | bytes 1572872 | tf_op jit(solution)/shard_map/ppermute | solution.py:30
  3.8 0.5 collective-permute-start.3
  4.3 1.9 %collective-permute-start.5 = (bf16[128,2048]{1,0:T(8,128)(2,1)}, bf16[128,2048]{1,0:T(8,128)(2,1)S(1)}, u32[]{:S(2)}, u32[]{:S(2)}) collective-permute-start(bf16[128,2048]{1,0:T(8,128)(2,1)} %refs_0_.1), channel_id=1, source_target_pairs={{0,192},{8,200},{16,208},{24,216},{32,224},{40,232},{48,240},{56,2... | collective-permute-start | bytes 1572872 | tf_op jit(solution)/shard_map/ppermute | solution.py:30
  6.2 0.7 concatenate.44
  7.0 5.9 %normalize.1.own_ref = bf16[3,2048,256]{2,1,0:T(8,128)(2,1)} custom-call(f32[768,2048]{1,0:T(8,128)} %h_ref.1, f32[1,2048]{1,0:T(1,128)} %bitcast.5), custom_call_target="tpu_custom_call" | custom-call | flops 6291456 | bytes 9437184 | tf_op jit(solution)/shard_map/normalize/pallas_call | solution.py:45
  13.4 2.4 %collective-permute-done.4.refs_3_ = bf16[128,2048]{1,0:T(8,128)(2,1)S(1)} collective-permute-done((bf16[128,2048]{1,0:T(8,128)(2,1)}, bf16[128,2048]{1,0:T(8,128)(2,1)S(1)}, u32[]{:S(2)}, u32[]{:S(2)}) %collective-permute-start.4) | collective-permute-done | bytes 524320 | tf_op jit(solution)/shard_map/ppermute | solution.py:30
  15.9 1.2 %collective-permute-done.3.refs_2_ = bf16[128,2048]{1,0:T(8,128)(2,1)S(1)} collective-permute-done((bf16[128,2048]{1,0:T(8,128)(2,1)}, bf16[128,2048]{1,0:T(8,128)(2,1)S(1)}, u32[]{:S(2)}, u32[]{:S(2)}) %collective-permute-start.3) | collective-permute-done | bytes 524320 | tf_op jit(solution)/shard_map/ppermute | solution.py:30
  17.5 1.6 %collective-permute-start.6 = (bf16[128,2048]{1,0:T(8,128)(2,1)S(1)}, bf16[128,2048]{1,0:T(8,128)(2,1)S(1)}, u32[]{:S(2)}, u32[]{:S(2)}) collective-permute-start(bf16[128,2048]{1,0:T(8,128)(2,1)S(1)} %get-tuple-element.25), channel_id=1, source_target_pairs={{0,16},{8,24},{16,32},{24,40},{32,48},{40,56},{48,0},{56,8},{64,80... | collective-permute-start | bytes 1572872 | tf_op jit(solution)/shard_map/ppermute | solution.py:30
  19.1 0.6 collective-permute-start.7
  19.7 1.6 %collective-permute-start.8 = (bf16[128,2048]{1,0:T(8,128)(2,1)S(1)}, bf16[128,2048]{1,0:T(8,128)(2,1)S(1)}, u32[]{:S(2)}, u32[]{:S(2)}) collective-permute-start(bf16[128,2048]{1,0:T(8,128)(2,1)S(1)} %get-tuple-element.24), channel_id=1, source_target_pairs={{0,64},{8,72},{16,80},{24,88},{32,96},{40,104},{48,112},{56,120},{... | collective-permute-start | bytes 1572872 | tf_op jit(solution)/shard_map/ppermute | solution.py:30
  21.3 1.7 %collective-permute-start.9 = (bf16[128,2048]{1,0:T(8,128)(2,1)S(1)}, bf16[128,2048]{1,0:T(8,128)(2,1)S(1)}, u32[]{:S(2)}, u32[]{:S(2)}) collective-permute-start(bf16[128,2048]{1,0:T(8,128)(2,1)S(1)} %get-tuple-element.22), channel_id=1, source_target_pairs={{0,192},{8,200},{16,208},{24,216},{32,224},{40,232},{48,240},{56,2... | collective-permute-start | bytes 1572872 | tf_op jit(solution)/shard_map/ppermute | solution.py:30
  23.1 6.5 %collective-permute-done.6.refs_0_ = bf16[128,2048]{1,0:T(8,128)(2,1)S(1)} collective-permute-done((bf16[128,2048]{1,0:T(8,128)(2,1)S(1)}, bf16[128,2048]{1,0:T(8,128)(2,1)S(1)}, u32[]{:S(2)}, u32[]{:S(2)}) %collective-permute-start.6) | collective-permute-done | bytes 524320 | tf_op jit(solution)/shard_map/ppermute | solution.py:30
  29.6 1.5 %collective-permute-start.10 = (bf16[64,2048]{1,0:T(8,128)(2,1)S(1)}, bf16[64,2048]{1,0:T(8,128)(2,1)S(1)}, u32[]{:S(2)}, u32[]{:S(2)}) collective-permute-start(bf16[64,2048]{1,0:T(8,128)(2,1)S(1)} %pad_maximum_fusion.8), channel_id=1, source_target_pairs={{0,16},{8,24},{16,32},{24,40},{32,48},{40,56},{48,0},{56,8},{64,80... | collective-permute-start | bytes 786440 | tf_op jit(solution)/shard_map/ppermute | solution.py:30
  31.1 1.2 %collective-permute-start.11 = (bf16[64,2048]{1,0:T(8,128)(2,1)S(1)}, bf16[64,2048]{1,0:T(8,128)(2,1)S(1)}, u32[]{:S(2)}, u32[]{:S(2)}) collective-permute-start(bf16[64,2048]{1,0:T(8,128)(2,1)S(1)} %pad_maximum_fusion.9), channel_id=1, source_target_pairs={{0,48},{8,56},{16,0},{24,8},{32,16},{40,24},{48,32},{56,40},{64,11... | collective-permute-start | bytes 786440 | tf_op jit(solution)/shard_map/ppermute | solution.py:30
  32.5 1.8 %collective-permute-start.12 = (bf16[64,2048]{1,0:T(8,128)(2,1)S(1)}, bf16[64,2048]{1,0:T(8,128)(2,1)S(1)}, u32[]{:S(2)}, u32[]{:S(2)}) collective-permute-start(bf16[64,2048]{1,0:T(8,128)(2,1)S(1)} %pad_maximum_fusion.10), channel_id=1, source_target_pairs={{0,64},{8,72},{16,80},{24,88},{32,96},{40,104},{48,112},{56,120},{... | collective-permute-start | bytes 786440 | tf_op jit(solution)/shard_map/ppermute | solution.py:30
  34.3 1.4 %collective-permute-start.14 = (bf16[32,2048]{1,0:T(8,128)(2,1)S(1)}, bf16[32,2048]{1,0:T(8,128)(2,1)S(1)}, u32[]{:S(2)}, u32[]{:S(2)}) collective-permute-start(bf16[32,2048]{1,0:T(8,128)(2,1)S(1)} %slice.104), channel_id=1, source_target_pairs={{0,64},{8,72},{16,80},{24,88},{32,96},{40,104},{48,112},{56,120},{... | collective-permute-start | bytes 393224 | tf_op jit(solution)/shard_map/ppermute | solution.py:30
  35.9 0.7 collective-permute-done.10.refs_4_
  36.6 2.4 %collective-permute-start.15 = (bf16[32,2048]{1,0:T(8,128)(2,1)S(1)}, bf16[32,2048]{1,0:T(8,128)(2,1)S(1)}, u32[]{:S(2)}, u32[]{:S(2)}) collective-permute-start(bf16[32,2048]{1,0:T(8,128)(2,1)S(1)} %slice.105), channel_id=1, source_target_pairs={{0,192},{8,200},{16,208},{24,216},{32,224},{40,232},{48,240},{56,2... | collective-permute-start | bytes 393224 | tf_op jit(solution)/shard_map/ppermute | solution.py:30
  39.0 1.5 %collective-permute-start.16 = (bf16[32,2048]{1,0:T(8,128)(2,1)S(1)}, bf16[32,2048]{1,0:T(8,128)(2,1)S(1)}, u32[]{:S(2)}, u32[]{:S(2)}) collective-permute-start(bf16[32,2048]{1,0:T(8,128)(2,1)S(1)} %slice.106), channel_id=1, source_target_pairs={{0,16},{8,24},{16,32},{24,40},{32,48},{40,56},{48,0},{56,8},{64,80... | collective-permute-start | bytes 393224 | tf_op jit(solution)/shard_map/ppermute | solution.py:30
  40.6 1.3 %collective-permute-start.13 = (bf16[64,2048]{1,0:T(8,128)(2,1)S(1)}, bf16[64,2048]{1,0:T(8,128)(2,1)S(1)}, u32[]{:S(2)}, u32[]{:S(2)}) collective-permute-start(bf16[64,2048]{1,0:T(8,128)(2,1)S(1)} %pad_maximum_fusion.11), channel_id=1, source_target_pairs={{0,192},{8,200},{16,208},{24,216},{32,224},{40,232},{48,240},{56,2... | collective-permute-start | bytes 786440 | tf_op jit(solution)/shard_map/ppermute | solution.py:30
  41.9 2.7 %collective-permute-start.17 = (bf16[32,2048]{1,0:T(8,128)(2,1)S(1)}, bf16[32,2048]{1,0:T(8,128)(2,1)S(1)}, u32[]{:S(2)}, u32[]{:S(2)}) collective-permute-start(bf16[32,2048]{1,0:T(8,128)(2,1)S(1)} %slice.107), channel_id=1, source_target_pairs={{0,48},{8,56},{16,0},{24,8},{32,16},{40,24},{48,32},{56,40},{64,11... | collective-permute-start | bytes 393224 | tf_op jit(solution)/shard_map/ppermute | solution.py:30
  44.7 1.1 collective-permute-start.22
  45.7 2.2 %collective-permute-start.23 = (bf16[32,2048]{1,0:T(8,128)(2,1)S(1)}, bf16[32,2048]{1,0:T(8,128)(2,1)S(1)}, u32[]{:S(2)}, u32[]{:S(2)}) collective-permute-start(bf16[32,2048]{1,0:T(8,128)(2,1)S(1)} %collective-permute-done.15.refs_9_), channel_id=1, source_target_pairs={{0,192},{8,200},{16,208},{24,216},{32,224},{40,232},{48,240},{56,2... | collective-permute-start | bytes 393224 | tf_op jit(solution)/shard_map/ppermute | solution.py:30
  48.2 7.8 %score.3.prev_ref = f32[6,4,256]{2,1,0:T(4,128)S(1)} custom-call(s32[4]{0:T(128)S(1)} %pad_add_fusion.place_ref, s32[6,1,256]{2,1,0:T(1,128)S(1)} %constant_dynamic-update-slice_fusion.goal_ref, f32[6,4,256]{2,1,0:T(4,128)S(1)} %broadcast_in_dim.2.prev_ref, bf16[3,2048,256]{2,1,0:T(8,128)(2,1)S(1)} %copy-done, ...), custom_call_target="tpu_custom_call" | custom-call | flops 4026531840 | bytes 8912896 | tf_op jit(solution)/shard_map/score/pallas_call | solution.py:152
  56.1 3.2 %collective-permute-start.19 = (bf16[96,2048]{1,0:T(8,128)(2,1)S(1)}, bf16[96,2048]{1,0:T(8,128)(2,1)S(1)}, u32[]{:S(2)}, u32[]{:S(2)}) collective-permute-start(bf16[96,2048]{1,0:T(8,128)(2,1)S(1)} %pad_maximum_fusion.5), channel_id=1, source_target_pairs={{0,192},{8,200},{16,208},{24,216},{32,224},{40,232},{48,240},{56,2... | collective-permute-start | bytes 1179656 | tf_op jit(solution)/shard_map/ppermute | solution.py:30
  59.3 2.4 %collective-permute-start.20 = (bf16[96,2048]{1,0:T(8,128)(2,1)S(1)}, bf16[96,2048]{1,0:T(8,128)(2,1)S(1)}, u32[]{:S(2)}, u32[]{:S(2)}) collective-permute-start(bf16[96,2048]{1,0:T(8,128)(2,1)S(1)} %pad_maximum_fusion.6), channel_id=1, source_target_pairs={{0,16},{8,24},{16,32},{24,40},{32,48},{40,56},{48,0},{56,8},{64,80... | collective-permute-start | bytes 1179656 | tf_op jit(solution)/shard_map/ppermute | solution.py:30
  62.0 3.2 %collective-permute-start.25 = (bf16[32,2048]{1,0:T(8,128)(2,1)S(1)}, bf16[32,2048]{1,0:T(8,128)(2,1)S(1)}, u32[]{:S(2)}, u32[]{:S(2)}) collective-permute-start(bf16[32,2048]{1,0:T(8,128)(2,1)S(1)} %collective-permute-done.17.refs_11_), channel_id=1, source_target_pairs={{0,48},{8,56},{16,0},{24,8},{32,16},{40,24},{48,32},{56,40},{64,11... | collective-permute-start | bytes 393224 | tf_op jit(solution)/shard_map/ppermute | solution.py:30
  65.2 10.8 %score.4.prev_ref = f32[6,4,256]{2,1,0:T(4,128)S(1)} custom-call(s32[4]{0:T(128)S(1)} %pad_add_fusion.place_ref, s32[6,1,256]{2,1,0:T(1,128)S(1)} %constant_dynamic-update-slice_fusion.goal_ref, f32[6,4,256]{2,1,0:T(4,128)S(1)} %score.3.prev_ref, bf16[3,2048,256]{2,1,0:T(8,128)(2,1)S(1)} %copy-done, bf16[3,2048,256]{2,1,0:T(8,128)(2,1)} %collective-permute-done.1.other_ref, ...), custom_call_target="tpu_custom_call" | custom-call | flops 5637144576 | bytes 9961472 | tf_op jit(solution)/shard_map/score/pallas_call | solution.py:152
  76.0 8.4 %score.5 = (f32[3,4,256]{2,1,0:T(4,128)S(1)}, f32[3,4,256]{2,1,0:T(4,128)S(1)}) custom-call(s32[4]{0:T(128)S(1)} %pad_add_fusion.place_ref, s32[6,1,256]{2,1,0:T(1,128)S(1)} %constant_dynamic-update-slice_fusion.goal_ref, f32[6,4,256]{2,1,0:T(4,128)S(1)} %score.4.prev_ref, bf16[3,2048,256]{2,1,0:T(8,128)(2,1)S(1)} %copy-done, ...), custom_call_target="tpu_custom_call" | custom-call | flops 3221225472 | bytes 8388608 | tf_op jit(solution)/shard_map/score/pallas_call | solution.py:152
  84.5 0.6 copy-done.1
  85.1 1.2 %collective-permute-done.26.b_ref = f32[3,4,256]{2,1,0:T(4,128)S(1)} collective-permute-done((f32[3,4,256]{2,1,0:T(4,128)S(1)}, f32[3,4,256]{2,1,0:T(4,128)S(1)}, u32[]{:S(2)}, u32[]{:S(2)}) %collective-permute-start.26) | collective-permute-done | bytes 12320 | tf_op jit(solution)/shard_map/ppermute | solution.py:34
  86.2 0.6 copy-done.10
  86.8 1.3 %merge.1.refs_0_ = f32[3,4,256]{2,1,0:T(4,128)} custom-call(f32[3,4,256]{2,1,0:T(4,128)} %copy-done.1, f32[3,4,256]{2,1,0:T(4,128)} %copy-done.10), custom_call_target="tpu_custom_call" | custom-call | tf_op jit(solution)/shard_map/merge/pallas_call | solution.py:189
  88.2 2.0 %collective-permute-start.27 = (f32[3,4,256]{2,1,0:T(4,128)}, f32[3,4,256]{2,1,0:T(4,128)S(1)}, u32[]{:S(2)}, u32[]{:S(2)}) collective-permute-start(f32[3,4,256]{2,1,0:T(4,128)} %merge.1.refs_0_), channel_id=1, source_target_pairs={{0,1},{1,2},{2,3},{3,4},{4,5},{5,6},{6,7},{7,0},{8,9},{9,10},{10,1... | collective-permute-start | bytes 36872 | tf_op jit(solution)/shard_map/ppermute | solution.py:307
  90.2 3.9 %collective-permute-start.28 = (f32[3,4,256]{2,1,0:T(4,128)}, f32[3,4,256]{2,1,0:T(4,128)S(1)}, u32[]{:S(2)}, u32[]{:S(2)}) collective-permute-start(f32[3,4,256]{2,1,0:T(4,128)} %merge.1.refs_0_), channel_id=1, source_target_pairs={{0,7},{1,0},{2,1},{3,2},{4,3},{5,4},{6,5},{7,6},{8,15},{9,8},{10,9... | collective-permute-start | bytes 36872 | tf_op jit(solution)/shard_map/ppermute | solution.py:310
  94.1 1.9 %collective-permute-done.27.refs_1_ = f32[3,4,256]{2,1,0:T(4,128)S(1)} collective-permute-done((f32[3,4,256]{2,1,0:T(4,128)}, f32[3,4,256]{2,1,0:T(4,128)S(1)}, u32[]{:S(2)}, u32[]{:S(2)}) %collective-permute-start.27) | collective-permute-done | bytes 12320 | tf_op jit(solution)/shard_map/ppermute | solution.py:307
  96.0 3.2 %collective-permute-start.30 = (f32[3,4,256]{2,1,0:T(4,128)S(1)}, f32[3,4,256]{2,1,0:T(4,128)S(1)}, u32[]{:S(2)}, u32[]{:S(2)}) collective-permute-start(f32[3,4,256]{2,1,0:T(4,128)S(1)} %collective-permute-done.28.refs_2_), channel_id=1, source_target_pairs={{0,7},{1,0},{2,1},{3,2},{4,3},{5,4},{6,5},{7,6},{8,15},{9,8},{10,9... | collective-permute-start | bytes 36872 | tf_op jit(solution)/shard_map/ppermute | solution.py:310
  99.3 1.7 %collective-permute-done.29.refs_3_ = f32[3,4,256]{2,1,0:T(4,128)S(1)} collective-permute-done((f32[3,4,256]{2,1,0:T(4,128)S(1)}, f32[3,4,256]{2,1,0:T(4,128)S(1)}, u32[]{:S(2)}, u32[]{:S(2)}) %collective-permute-start.29) | collective-permute-done | bytes 12320 | tf_op jit(solution)/shard_map/ppermute | solution.py:307
  100.9 3.2 %collective-permute-start.32 = (f32[3,4,256]{2,1,0:T(4,128)S(1)}, f32[3,4,256]{2,1,0:T(4,128)S(1)}, u32[]{:S(2)}, u32[]{:S(2)}) collective-permute-start(f32[3,4,256]{2,1,0:T(4,128)S(1)} %collective-permute-done.30.refs_4_), channel_id=1, source_target_pairs={{0,7},{1,0},{2,1},{3,2},{4,3},{5,4},{6,5},{7,6},{8,15},{9,8},{10,9... | collective-permute-start | bytes 36872 | tf_op jit(solution)/shard_map/ppermute | solution.py:310
  104.2 1.7 %collective-permute-done.31.refs_5_ = f32[3,4,256]{2,1,0:T(4,128)S(1)} collective-permute-done((f32[3,4,256]{2,1,0:T(4,128)S(1)}, f32[3,4,256]{2,1,0:T(4,128)S(1)}, u32[]{:S(2)}, u32[]{:S(2)}) %collective-permute-start.31) | collective-permute-done | bytes 12320 | tf_op jit(solution)/shard_map/ppermute | solution.py:307
  106.5 4.2 %collective-permute-done.33.refs_7_ = f32[3,4,256]{2,1,0:T(4,128)S(1)} collective-permute-done((f32[3,4,256]{2,1,0:T(4,128)S(1)}, f32[3,4,256]{2,1,0:T(4,128)S(1)}, u32[]{:S(2)}, u32[]{:S(2)}) %collective-permute-start.33) | collective-permute-done | bytes 12320 | tf_op jit(solution)/shard_map/ppermute | solution.py:307
  110.8 0.6 copy-done.9
  111.4 1.5 %finish.1 = (f32[3,1,256]{2,1,0:T(1,128)}, f32[3,1,256]{2,1,0:T(1,128)}) custom-call(s32[1]{0:T(128)S(6)} %copy.8.length_ref, f32[3,4,256]{2,1,0:T(4,128)} %merge.1.refs_0_, f32[3,4,256]{2,1,0:T(4,128)} %copy-done.3, f32[3,4,256]{2,1,0:T(4,128)} %copy-done.4, f32[3,4,256]{2,1,0:T(4,128)} %copy-done.5, f32[3,4,256]{2,1,0:T(4,128)} %copy-done.6, ...), custom_call_target="tpu_custom_call" | custom-call | tf_op jit(solution)/shard_map/finish/pallas_call | solution.py:206
  112.8 0.7 reduce
  113.5 0.6 reshape.18
  114.1 0.7 reduce.1
  114.8 0.6 reshape.19
  (82 shorter events, 2.2 us)
Async XLA Ops:
  0.6 15.2 %collective-permute-start.4 = (bf16[128,2048]{1,0:T(8,128)(2,1)}, bf16[128,2048]{1,0:T(8,128)(2,1)S(1)}, u32[]{:S(2)}, u32[]{:S(2)}) collective-permute-start(bf16[128,2048]{1,0:T(8,128)(2,1)} %refs_0_.1), channel_id=1, source_target_pairs={{0,64},{8,72},{16,80},{24,88},{32,96},{40,104},{48,112},{56,120},{... | collective-permute-start | bytes 1572872 | tf_op jit(solution)/shard_map/ppermute | solution.py:30
  2.3 14.8 %collective-permute-start.2 = (bf16[128,2048]{1,0:T(8,128)(2,1)}, bf16[128,2048]{1,0:T(8,128)(2,1)S(1)}, u32[]{:S(2)}, u32[]{:S(2)}) collective-permute-start(bf16[128,2048]{1,0:T(8,128)(2,1)} %refs_0_.1), channel_id=1, source_target_pairs={{0,16},{8,24},{16,32},{24,40},{32,48},{40,56},{48,0},{56,8},{64,80... | collective-permute-start | bytes 1572872 | tf_op jit(solution)/shard_map/ppermute | solution.py:30
  3.8 13.3 %collective-permute-start.3 = (bf16[128,2048]{1,0:T(8,128)(2,1)}, bf16[128,2048]{1,0:T(8,128)(2,1)S(1)}, u32[]{:S(2)}, u32[]{:S(2)}) collective-permute-start(bf16[128,2048]{1,0:T(8,128)(2,1)} %refs_0_.1), channel_id=1, source_target_pairs={{0,48},{8,56},{16,0},{24,8},{32,16},{40,24},{48,32},{56,40},{64,11... | collective-permute-start | bytes 1572872 | tf_op jit(solution)/shard_map/ppermute | solution.py:30
  4.3 13.0 %collective-permute-start.5 = (bf16[128,2048]{1,0:T(8,128)(2,1)}, bf16[128,2048]{1,0:T(8,128)(2,1)S(1)}, u32[]{:S(2)}, u32[]{:S(2)}) collective-permute-start(bf16[128,2048]{1,0:T(8,128)(2,1)} %refs_0_.1), channel_id=1, source_target_pairs={{0,192},{8,200},{16,208},{24,216},{32,224},{40,232},{48,240},{56,2... | collective-permute-start | bytes 1572872 | tf_op jit(solution)/shard_map/ppermute | solution.py:30
  6.2 6.7 %collective-permute-start = (s32[768]{0:T(1024)}, s32[768]{0:T(1024)S(1)}, u32[]{:S(2)}, u32[]{:S(2)}) collective-permute-start(s32[768]{0:T(1024)} %param.8), channel_id=1, source_target_pairs={{0,8},{8,0},{16,24},{24,16},{32,40},{40,32},{48,56},{56,48},{64,72... | collective-permute-start | bytes 9224 | tf_op jit(solution)/shard_map/ppermute | solution.py:34
  12.9 35.0 %collective-permute-start.1 = (bf16[3,2048,256]{2,1,0:T(8,128)(2,1)}, bf16[3,2048,256]{2,1,0:T(8,128)(2,1)}, u32[]{:S(2)}, u32[]{:S(2)}) collective-permute-start(bf16[3,2048,256]{2,1,0:T(8,128)(2,1)} %normalize.1.own_ref), channel_id=1, source_target_pairs={{0,8},{8,0},{16,24},{24,16},{32,40},{40,32},{48,56},{56,48},{64,72... | collective-permute-start | bytes 9437192 | tf_op jit(solution)/shard_map/ppermute | solution.py:34
  17.5 12.2 %collective-permute-start.6 = (bf16[128,2048]{1,0:T(8,128)(2,1)S(1)}, bf16[128,2048]{1,0:T(8,128)(2,1)S(1)}, u32[]{:S(2)}, u32[]{:S(2)}) collective-permute-start(bf16[128,2048]{1,0:T(8,128)(2,1)S(1)} %get-tuple-element.25), channel_id=1, source_target_pairs={{0,16},{8,24},{16,32},{24,40},{32,48},{40,56},{48,0},{56,8},{64,80... | collective-permute-start | bytes 1572872 | tf_op jit(solution)/shard_map/ppermute | solution.py:30
  19.1 12.0 %collective-permute-start.7 = (bf16[128,2048]{1,0:T(8,128)(2,1)S(1)}, bf16[128,2048]{1,0:T(8,128)(2,1)S(1)}, u32[]{:S(2)}, u32[]{:S(2)}) collective-permute-start(bf16[128,2048]{1,0:T(8,128)(2,1)S(1)} %get-tuple-element.23), channel_id=1, source_target_pairs={{0,48},{8,56},{16,0},{24,8},{32,16},{40,24},{48,32},{56,40},{64,11... | collective-permute-start | bytes 1572872 | tf_op jit(solution)/shard_map/ppermute | solution.py:30
  19.7 12.7 %collective-permute-start.8 = (bf16[128,2048]{1,0:T(8,128)(2,1)S(1)}, bf16[128,2048]{1,0:T(8,128)(2,1)S(1)}, u32[]{:S(2)}, u32[]{:S(2)}) collective-permute-start(bf16[128,2048]{1,0:T(8,128)(2,1)S(1)} %get-tuple-element.24), channel_id=1, source_target_pairs={{0,64},{8,72},{16,80},{24,88},{32,96},{40,104},{48,112},{56,120},{... | collective-permute-start | bytes 1572872 | tf_op jit(solution)/shard_map/ppermute | solution.py:30
  21.3 13.0 %collective-permute-start.9 = (bf16[128,2048]{1,0:T(8,128)(2,1)S(1)}, bf16[128,2048]{1,0:T(8,128)(2,1)S(1)}, u32[]{:S(2)}, u32[]{:S(2)}) collective-permute-start(bf16[128,2048]{1,0:T(8,128)(2,1)S(1)} %get-tuple-element.22), channel_id=1, source_target_pairs={{0,192},{8,200},{16,208},{24,216},{32,224},{40,232},{48,240},{56,2... | collective-permute-start | bytes 1572872 | tf_op jit(solution)/shard_map/ppermute | solution.py:30
  23.1 25.0 %copy-start.11 = (f32[4]{0:T(128)S(1)}, f32[4]{0:T(128)}, u32[]{:S(2)}) copy-start(f32[4]{0:T(128)} %constant.57.clone.1) | copy-start | bytes 52
  23.1 25.1 %copy-start = (bf16[3,2048,256]{2,1,0:T(8,128)(2,1)S(1)}, bf16[3,2048,256]{2,1,0:T(8,128)(2,1)}, u32[]{:S(2)}) copy-start(bf16[3,2048,256]{2,1,0:T(8,128)(2,1)} %normalize.1.own_ref) | copy-start | bytes 9437188
  23.1 25.1 %copy-start.2 = (bf16[128,2048]{1,0:T(8,128)(2,1)S(1)}, bf16[128,2048]{1,0:T(8,128)(2,1)}, u32[]{:S(2)}) copy-start(bf16[128,2048]{1,0:T(8,128)(2,1)} %refs_0_.1) | copy-start | bytes 1572868
  29.6 7.0 %collective-permute-start.10 = (bf16[64,2048]{1,0:T(8,128)(2,1)S(1)}, bf16[64,2048]{1,0:T(8,128)(2,1)S(1)}, u32[]{:S(2)}, u32[]{:S(2)}) collective-permute-start(bf16[64,2048]{1,0:T(8,128)(2,1)S(1)} %pad_maximum_fusion.8), channel_id=1, source_target_pairs={{0,16},{8,24},{16,32},{24,40},{32,48},{40,56},{48,0},{56,8},{64,80... | collective-permute-start | bytes 786440 | tf_op jit(solution)/shard_map/ppermute | solution.py:30
  31.1 7.9 %collective-permute-start.11 = (bf16[64,2048]{1,0:T(8,128)(2,1)S(1)}, bf16[64,2048]{1,0:T(8,128)(2,1)S(1)}, u32[]{:S(2)}, u32[]{:S(2)}) collective-permute-start(bf16[64,2048]{1,0:T(8,128)(2,1)S(1)} %pad_maximum_fusion.9), channel_id=1, source_target_pairs={{0,48},{8,56},{16,0},{24,8},{32,16},{40,24},{48,32},{56,40},{64,11... | collective-permute-start | bytes 786440 | tf_op jit(solution)/shard_map/ppermute | solution.py:30
  32.5 8.1 %collective-permute-start.12 = (bf16[64,2048]{1,0:T(8,128)(2,1)S(1)}, bf16[64,2048]{1,0:T(8,128)(2,1)S(1)}, u32[]{:S(2)}, u32[]{:S(2)}) collective-permute-start(bf16[64,2048]{1,0:T(8,128)(2,1)S(1)} %pad_maximum_fusion.10), channel_id=1, source_target_pairs={{0,64},{8,72},{16,80},{24,88},{32,96},{40,104},{48,112},{56,120},{... | collective-permute-start | bytes 786440 | tf_op jit(solution)/shard_map/ppermute | solution.py:30
  34.3 7.7 %collective-permute-start.14 = (bf16[32,2048]{1,0:T(8,128)(2,1)S(1)}, bf16[32,2048]{1,0:T(8,128)(2,1)S(1)}, u32[]{:S(2)}, u32[]{:S(2)}) collective-permute-start(bf16[32,2048]{1,0:T(8,128)(2,1)S(1)} %slice.104), channel_id=1, source_target_pairs={{0,64},{8,72},{16,80},{24,88},{32,96},{40,104},{48,112},{56,120},{... | collective-permute-start | bytes 393224 | tf_op jit(solution)/shard_map/ppermute | solution.py:30
  36.6 8.1 %collective-permute-start.15 = (bf16[32,2048]{1,0:T(8,128)(2,1)S(1)}, bf16[32,2048]{1,0:T(8,128)(2,1)S(1)}, u32[]{:S(2)}, u32[]{:S(2)}) collective-permute-start(bf16[32,2048]{1,0:T(8,128)(2,1)S(1)} %slice.105), channel_id=1, source_target_pairs={{0,192},{8,200},{16,208},{24,216},{32,224},{40,232},{48,240},{56,2... | collective-permute-start | bytes 393224 | tf_op jit(solution)/shard_map/ppermute | solution.py:30
  39.0 6.7 %collective-permute-start.16 = (bf16[32,2048]{1,0:T(8,128)(2,1)S(1)}, bf16[32,2048]{1,0:T(8,128)(2,1)S(1)}, u32[]{:S(2)}, u32[]{:S(2)}) collective-permute-start(bf16[32,2048]{1,0:T(8,128)(2,1)S(1)} %slice.106), channel_id=1, source_target_pairs={{0,16},{8,24},{16,32},{24,40},{32,48},{40,56},{48,0},{56,8},{64,80... | collective-permute-start | bytes 393224 | tf_op jit(solution)/shard_map/ppermute | solution.py:30
  40.6 15.4 %collective-permute-start.13 = (bf16[64,2048]{1,0:T(8,128)(2,1)S(1)}, bf16[64,2048]{1,0:T(8,128)(2,1)S(1)}, u32[]{:S(2)}, u32[]{:S(2)}) collective-permute-start(bf16[64,2048]{1,0:T(8,128)(2,1)S(1)} %pad_maximum_fusion.11), channel_id=1, source_target_pairs={{0,192},{8,200},{16,208},{24,216},{32,224},{40,232},{48,240},{56,2... | collective-permute-start | bytes 786440 | tf_op jit(solution)/shard_map/ppermute | solution.py:30
  41.9 14.2 %collective-permute-start.17 = (bf16[32,2048]{1,0:T(8,128)(2,1)S(1)}, bf16[32,2048]{1,0:T(8,128)(2,1)S(1)}, u32[]{:S(2)}, u32[]{:S(2)}) collective-permute-start(bf16[32,2048]{1,0:T(8,128)(2,1)S(1)} %slice.107), channel_id=1, source_target_pairs={{0,48},{8,56},{16,0},{24,8},{32,16},{40,24},{48,32},{56,40},{64,11... | collective-permute-start | bytes 393224 | tf_op jit(solution)/shard_map/ppermute | solution.py:30
  44.7 14.7 %collective-permute-start.22 = (bf16[32,2048]{1,0:T(8,128)(2,1)S(1)}, bf16[32,2048]{1,0:T(8,128)(2,1)S(1)}, u32[]{:S(2)}, u32[]{:S(2)}) collective-permute-start(bf16[32,2048]{1,0:T(8,128)(2,1)S(1)} %collective-permute-done.14.refs_8_), channel_id=1, source_target_pairs={{0,64},{8,72},{16,80},{24,88},{32,96},{40,104},{48,112},{56,120},{... | collective-permute-start | bytes 393224 | tf_op jit(solution)/shard_map/ppermute | solution.py:30
  45.7 16.0 %collective-permute-start.23 = (bf16[32,2048]{1,0:T(8,128)(2,1)S(1)}, bf16[32,2048]{1,0:T(8,128)(2,1)S(1)}, u32[]{:S(2)}, u32[]{:S(2)}) collective-permute-start(bf16[32,2048]{1,0:T(8,128)(2,1)S(1)} %collective-permute-done.15.refs_9_), channel_id=1, source_target_pairs={{0,192},{8,200},{16,208},{24,216},{32,224},{40,232},{48,240},{56,2... | collective-permute-start | bytes 393224 | tf_op jit(solution)/shard_map/ppermute | solution.py:30
  47.9 14.1 %collective-permute-start.24 = (bf16[32,2048]{1,0:T(8,128)(2,1)S(1)}, bf16[32,2048]{1,0:T(8,128)(2,1)S(1)}, u32[]{:S(2)}, u32[]{:S(2)}) collective-permute-start(bf16[32,2048]{1,0:T(8,128)(2,1)S(1)} %collective-permute-done.16.refs_10_), channel_id=1, source_target_pairs={{0,16},{8,24},{16,32},{24,40},{32,48},{40,56},{48,0},{56,8},{64,80... | collective-permute-start | bytes 393224 | tf_op jit(solution)/shard_map/ppermute | solution.py:30
  56.0 20.0 %collective-permute-start.18 = (bf16[96,2048]{1,0:T(8,128)(2,1)S(1)}, bf16[96,2048]{1,0:T(8,128)(2,1)S(1)}, u32[]{:S(2)}, u32[]{:S(2)}) collective-permute-start(bf16[96,2048]{1,0:T(8,128)(2,1)S(1)} %pad_maximum_fusion.4), channel_id=1, source_target_pairs={{0,64},{8,72},{16,80},{24,88},{32,96},{40,104},{48,112},{56,120},{... | collective-permute-start | bytes 1179656 | tf_op jit(solution)/shard_map/ppermute | solution.py:30
  56.1 19.9 %collective-permute-start.19 = (bf16[96,2048]{1,0:T(8,128)(2,1)S(1)}, bf16[96,2048]{1,0:T(8,128)(2,1)S(1)}, u32[]{:S(2)}, u32[]{:S(2)}) collective-permute-start(bf16[96,2048]{1,0:T(8,128)(2,1)S(1)} %pad_maximum_fusion.5), channel_id=1, source_target_pairs={{0,192},{8,200},{16,208},{24,216},{32,224},{40,232},{48,240},{56,2... | collective-permute-start | bytes 1179656 | tf_op jit(solution)/shard_map/ppermute | solution.py:30
  59.3 16.7 %collective-permute-start.20 = (bf16[96,2048]{1,0:T(8,128)(2,1)S(1)}, bf16[96,2048]{1,0:T(8,128)(2,1)S(1)}, u32[]{:S(2)}, u32[]{:S(2)}) collective-permute-start(bf16[96,2048]{1,0:T(8,128)(2,1)S(1)} %pad_maximum_fusion.6), channel_id=1, source_target_pairs={{0,16},{8,24},{16,32},{24,40},{32,48},{40,56},{48,0},{56,8},{64,80... | collective-permute-start | bytes 1179656 | tf_op jit(solution)/shard_map/ppermute | solution.py:30
  61.7 14.3 %collective-permute-start.21 = (bf16[96,2048]{1,0:T(8,128)(2,1)S(1)}, bf16[96,2048]{1,0:T(8,128)(2,1)S(1)}, u32[]{:S(2)}, u32[]{:S(2)}) collective-permute-start(bf16[96,2048]{1,0:T(8,128)(2,1)S(1)} %pad_maximum_fusion.7), channel_id=1, source_target_pairs={{0,48},{8,56},{16,0},{24,8},{32,16},{40,24},{48,32},{56,40},{64,11... | collective-permute-start | bytes 1179656 | tf_op jit(solution)/shard_map/ppermute | solution.py:30
  62.0 14.0 %collective-permute-start.25 = (bf16[32,2048]{1,0:T(8,128)(2,1)S(1)}, bf16[32,2048]{1,0:T(8,128)(2,1)S(1)}, u32[]{:S(2)}, u32[]{:S(2)}) collective-permute-start(bf16[32,2048]{1,0:T(8,128)(2,1)S(1)} %collective-permute-done.17.refs_11_), channel_id=1, source_target_pairs={{0,48},{8,56},{16,0},{24,8},{32,16},{40,24},{48,32},{56,40},{64,11... | collective-permute-start | bytes 393224 | tf_op jit(solution)/shard_map/ppermute | solution.py:30
  84.5 0.6 copy-start.1
  85.1 1.2 %collective-permute-start.26 = (f32[3,4,256]{2,1,0:T(4,128)S(1)}, f32[3,4,256]{2,1,0:T(4,128)S(1)}, u32[]{:S(2)}, u32[]{:S(2)}) collective-permute-start(f32[3,4,256]{2,1,0:T(4,128)S(1)} %get-tuple-element.7), channel_id=1, source_target_pairs={{0,8},{8,0},{16,24},{24,16},{32,40},{40,32},{48,56},{56,48},{64,72... | collective-permute-start | bytes 36872 | tf_op jit(solution)/shard_map/ppermute | solution.py:34
  86.2 0.6 copy-start.10
  88.2 7.8 %collective-permute-start.27 = (f32[3,4,256]{2,1,0:T(4,128)}, f32[3,4,256]{2,1,0:T(4,128)S(1)}, u32[]{:S(2)}, u32[]{:S(2)}) collective-permute-start(f32[3,4,256]{2,1,0:T(4,128)} %merge.1.refs_0_), channel_id=1, source_target_pairs={{0,1},{1,2},{2,3},{3,4},{4,5},{5,6},{6,7},{7,0},{8,9},{9,10},{10,1... | collective-permute-start | bytes 36872 | tf_op jit(solution)/shard_map/ppermute | solution.py:307
  90.2 5.8 %collective-permute-start.28 = (f32[3,4,256]{2,1,0:T(4,128)}, f32[3,4,256]{2,1,0:T(4,128)S(1)}, u32[]{:S(2)}, u32[]{:S(2)}) collective-permute-start(f32[3,4,256]{2,1,0:T(4,128)} %merge.1.refs_0_), channel_id=1, source_target_pairs={{0,7},{1,0},{2,1},{3,2},{4,3},{5,4},{6,5},{7,6},{8,15},{9,8},{10,9... | collective-permute-start | bytes 36872 | tf_op jit(solution)/shard_map/ppermute | solution.py:310
  96.0 14.7 %copy-start.3 = (f32[3,4,256]{2,1,0:T(4,128)}, f32[3,4,256]{2,1,0:T(4,128)S(1)}, u32[]{:S(2)}) copy-start(f32[3,4,256]{2,1,0:T(4,128)S(1)} %collective-permute-done.27.refs_1_) | copy-start | bytes 36868
  96.0 4.9 %collective-permute-start.29 = (f32[3,4,256]{2,1,0:T(4,128)S(1)}, f32[3,4,256]{2,1,0:T(4,128)S(1)}, u32[]{:S(2)}, u32[]{:S(2)}) collective-permute-start(f32[3,4,256]{2,1,0:T(4,128)S(1)} %collective-permute-done.27.refs_1_), channel_id=1, source_target_pairs={{0,1},{1,2},{2,3},{3,4},{4,5},{5,6},{6,7},{7,0},{8,9},{9,10},{10,1... | collective-permute-start | bytes 36872 | tf_op jit(solution)/shard_map/ppermute | solution.py:307
  96.0 14.7 %copy-start.4 = (f32[3,4,256]{2,1,0:T(4,128)}, f32[3,4,256]{2,1,0:T(4,128)S(1)}, u32[]{:S(2)}) copy-start(f32[3,4,256]{2,1,0:T(4,128)S(1)} %collective-permute-done.28.refs_2_) | copy-start | bytes 36868
  96.0 4.9 %collective-permute-start.30 = (f32[3,4,256]{2,1,0:T(4,128)S(1)}, f32[3,4,256]{2,1,0:T(4,128)S(1)}, u32[]{:S(2)}, u32[]{:S(2)}) collective-permute-start(f32[3,4,256]{2,1,0:T(4,128)S(1)} %collective-permute-done.28.refs_2_), channel_id=1, source_target_pairs={{0,7},{1,0},{2,1},{3,2},{4,3},{5,4},{6,5},{7,6},{8,15},{9,8},{10,9... | collective-permute-start | bytes 36872 | tf_op jit(solution)/shard_map/ppermute | solution.py:310
  100.9 9.8 %copy-start.5 = (f32[3,4,256]{2,1,0:T(4,128)}, f32[3,4,256]{2,1,0:T(4,128)S(1)}, u32[]{:S(2)}) copy-start(f32[3,4,256]{2,1,0:T(4,128)S(1)} %collective-permute-done.29.refs_3_) | copy-start | bytes 36868
  100.9 4.9 %collective-permute-start.31 = (f32[3,4,256]{2,1,0:T(4,128)S(1)}, f32[3,4,256]{2,1,0:T(4,128)S(1)}, u32[]{:S(2)}, u32[]{:S(2)}) collective-permute-start(f32[3,4,256]{2,1,0:T(4,128)S(1)} %collective-permute-done.29.refs_3_), channel_id=1, source_target_pairs={{0,1},{1,2},{2,3},{3,4},{4,5},{5,6},{6,7},{7,0},{8,9},{9,10},{10,1... | collective-permute-start | bytes 36872 | tf_op jit(solution)/shard_map/ppermute | solution.py:307
  100.9 9.8 %copy-start.6 = (f32[3,4,256]{2,1,0:T(4,128)}, f32[3,4,256]{2,1,0:T(4,128)S(1)}, u32[]{:S(2)}) copy-start(f32[3,4,256]{2,1,0:T(4,128)S(1)} %collective-permute-done.30.refs_4_) | copy-start | bytes 36868
  100.9 5.6 %collective-permute-start.32 = (f32[3,4,256]{2,1,0:T(4,128)S(1)}, f32[3,4,256]{2,1,0:T(4,128)S(1)}, u32[]{:S(2)}, u32[]{:S(2)}) collective-permute-start(f32[3,4,256]{2,1,0:T(4,128)S(1)} %collective-permute-done.30.refs_4_), channel_id=1, source_target_pairs={{0,7},{1,0},{2,1},{3,2},{4,3},{5,4},{6,5},{7,6},{8,15},{9,8},{10,9... | collective-permute-start | bytes 36872 | tf_op jit(solution)/shard_map/ppermute | solution.py:310
  105.8 4.9 %copy-start.7 = (f32[3,4,256]{2,1,0:T(4,128)}, f32[3,4,256]{2,1,0:T(4,128)S(1)}, u32[]{:S(2)}) copy-start(f32[3,4,256]{2,1,0:T(4,128)S(1)} %collective-permute-done.31.refs_5_) | copy-start | bytes 36868
  105.8 4.9 %collective-permute-start.33 = (f32[3,4,256]{2,1,0:T(4,128)S(1)}, f32[3,4,256]{2,1,0:T(4,128)S(1)}, u32[]{:S(2)}, u32[]{:S(2)}) collective-permute-start(f32[3,4,256]{2,1,0:T(4,128)S(1)} %collective-permute-done.31.refs_5_), channel_id=1, source_target_pairs={{0,1},{1,2},{2,3},{3,4},{4,5},{5,6},{6,7},{7,0},{8,9},{9,10},{10,1... | collective-permute-start | bytes 36872 | tf_op jit(solution)/shard_map/ppermute | solution.py:307
  106.5 4.3 %copy-start.8 = (f32[3,4,256]{2,1,0:T(4,128)}, f32[3,4,256]{2,1,0:T(4,128)S(1)}, u32[]{:S(2)}) copy-start(f32[3,4,256]{2,1,0:T(4,128)S(1)} %collective-permute-done.32.refs_6_) | copy-start | bytes 36868
  110.8 0.6 copy-start.9
